TPU v7x, 256 devices: a whole 4x4x8 slice. The times are simulated.
256 devices in a mesh: sec: 64 (over z, x, core), op: 4 (over y).
Axes of the slice: x: 4, y: 4, z: 8, core: 2. Of those that a mesh axis runs over, the one named last changes fastest.
Arguments:
- wavefunction: bfloat16 [4096, 128, 128], P('sec'), may hold values from -6 to 6
- sector_left: int32 [4096], P('sec'), may hold values from 0 to 127, as said below
- sector_right: int32 [4096], replicated, may hold values from 0 to 127, as said below
- left_sizes: int32 [128], replicated, may hold values from 64 to 128
- right_sizes: int32 [128], replicated, may hold values from 64 to 128
- term_mask: int32 [16, 4096], P('op', 'sec'), may hold values 0 or 1
- left_environment: bfloat16 [16, 128, 128, 128], P('op', 'sec'), may hold values from -0.5 to 0.5
- right_environment: bfloat16 [16, 128, 128, 128], P('op', 'sec'), may hold values from -0.5 to 0.5
- krylov_basis: bfloat16 [4, 4096, 128, 128], P(None, 'sec', 'op')
Outputs:
- applied_wave: bfloat16 [4096, 128, 128], P('sec', 'op')
- correlations: float32 [4], replicated
Inputs may be any that keep to these rules, and one draw needn't show every extreme that they name: `sector_left`: sector s has one of the 2 left numbers 2 * (s // 64) to 2 * (s // 64) + 1. `sector_right`: right number q is owned by index q // 2 of sec. No two sectors among the 64 of one device share a right number; at most 2 of them share a right owner, and in every draw some owner receives 2 sectors from every device. Right numbers 0 to 127 are drawn, and 127 is used in every draw.
All inputs are finite; a program needn't handle non-finite values. No bound on the sum of `term_mask` on one device may be relied on, other than what follows from the above.
Results may differ from a plain program's by a relative error of at most 0.0049.
Values may be sent and summed in bfloat16 or wider, within the bound.
A program may use at most 256 MiB of HBM per device.

v0:
```python
import jax
import jax.numpy as jnp
from jax import lax
from jax.sharding import PartitionSpec as P

RQ_DEV = 2
CAP = 2


def lookup_small(keys, table):
    table_index = jnp.arange(table.shape[0], dtype=jnp.int32)
    return jnp.sum(jnp.where(keys[:, None] == table_index[None, :], table[None, :], 0), axis=1)


def per_device(
    wavefunction,
    sector_left,
    sector_right,
    left_sizes,
    right_sizes,
    term_mask,
    left_environment,
    right_environment,
    krylov_basis,
):
    holders = lax.axis_size("sec")
    holder = lax.axis_index("sec")
    sector_count = wavefunction.shape[0]
    tile_size = wavefunction.shape[1]
    left_per = left_environment.shape[1]
    right_per = right_environment.shape[1]
    slot_total = holders * CAP
    all_right = sector_right.reshape(holders, sector_count)
    owners = all_right // RQ_DEV
    positions = jnp.arange(sector_count, dtype=jnp.int32)
    before = positions[None, :] < positions[:, None]
    shared = owners[:, :, None] == owners[:, None, :]
    rank_of = jnp.sum(shared & before[None], axis=2)
    slot_of = owners * CAP + rank_of
    my_slot = lax.dynamic_index_in_dim(slot_of, holder, 0, keepdims=False)
    my_right = lax.dynamic_slice_in_dim(sector_right, holder * sector_count, sector_count)
    lane_index = jnp.arange(tile_size, dtype=jnp.int32)
    left_size = lookup_small(sector_left, left_sizes)
    right_size = lookup_small(my_right, right_sizes)
    rows_inside = lane_index[None, :] < left_size[:, None]
    cols_inside = lane_index[None, :] < right_size[:, None]
    inside = rows_inside[:, :, None] & cols_inside[:, None, :]
    masked_psi = jnp.where(inside, wavefunction, jnp.zeros((), jnp.bfloat16))
    left_index = sector_left - holder * left_per
    slot_index = jnp.arange(slot_total, dtype=jnp.int32)
    slot_match = my_slot[:, None] == slot_index[None, :]
    slot_sector = jnp.sum(jnp.where(slot_match, positions[:, None], 0), axis=0)
    slot_used = jnp.any(slot_match, axis=0)
    slot_ids = jnp.where(slot_used, jnp.take(my_right, slot_sector), -1).reshape(holders, CAP)
    term_count = left_environment.shape[0]
    left_tiles = jnp.take(left_environment, left_index, axis=1)
    product = jnp.einsum(
        "wsij,sjk->swik", left_tiles, masked_psi, preferred_element_type=jnp.float32
    )
    term_weight = term_mask.T.astype(jnp.float32)[:, :, None, None]
    row_lane = jnp.arange(tile_size, dtype=jnp.int32)
    row_weight = (row_lane[None, :] < left_size[:, None]).astype(jnp.float32)[:, None, :, None]
    left_part = (product * term_weight * row_weight).astype(jnp.bfloat16)
    outbound = jnp.take(left_part, slot_sector, axis=0).reshape(
        holders, CAP, term_count, tile_size, tile_size
    )
    tile_set = lax.all_to_all(outbound, "sec", split_axis=0, concat_axis=0, tiled=True)
    number_set = lax.all_to_all(slot_ids, "sec", split_axis=0, concat_axis=0, tiled=True)
    sources = tile_set.shape[0]
    slot_count = tile_set.shape[1]
    terms_here = right_environment.shape[0]
    local_index = jnp.clip(number_set - holder * right_per, 0, right_per - 1)
    env_tiles = jnp.take(right_environment, local_index.reshape(-1), axis=1)
    env_tiles = env_tiles.reshape(terms_here, sources, slot_count, tile_size, tile_size)
    partial_value = jnp.einsum(
        "ncwij,wnckj->ncik", tile_set, env_tiles, preferred_element_type=jnp.float32
    )
    shares = lax.psum_scatter(partial_value, "op", scatter_dimension=2, tiled=True).astype(
        jnp.bfloat16
    )
    returned = lax.all_to_all(shares, "sec", split_axis=0, concat_axis=0, tiled=True)
    result_rows = jnp.take(
        returned.reshape(slot_total, shares.shape[2], tile_size), my_slot, axis=0
    )
    applied_wave = jnp.where(cols_inside[:, None, :], result_rows, jnp.zeros((), jnp.bfloat16))
    local_sum = jnp.einsum(
        "ksij,sij->k", krylov_basis, applied_wave, preferred_element_type=jnp.float32
    )
    correlations = lax.psum(local_sum, ("sec", "op"))
    return (applied_wave, correlations)


def solution(mesh):
    return jax.shard_map(
        per_device,
        mesh=mesh,
        in_specs=(
            P("sec", None, None),
            P("sec"),
            P(),
            P(),
            P(),
            P("op", "sec"),
            P("op", "sec", None, None),
            P("op", "sec", None, None),
            P(None, "sec", "op", None),
        ),
        out_specs=(P("sec", "op", None), P()),
        check_vma=False,
    )
```

profile of v0, /device:TPU:1, one launch (start us, length us, event | category | flops | bytes accessed | tf_op | source)
XLA Modules:
  0.0 682.6 jit_solution(16601726818128462754)
XLA Ops:
  7.2 0.9 reshape.310
  8.2 1.9 convert_reduce_fusion
  10.0 0.7 compare_and_fusion.2
  10.8 0.1 reduce_sum.48
  11.0 0.8 dynamic_slice.7
  11.8 1.2 gather_fusion.2
  13.2 0.2 reduce_or.12
  13.3 0.6 select_select_fusion.1
  14.0 13.0 %all-to-all-start.1 = ((s32[64,1,2]{2,1,0:T(1,128)}), s32[64,1,2]{2,1,0:T(1,128)S(1)}, u32[]{:S(2)}, u32[]{:S(2)}) async-start(s32[64,1,2]{2,1,0:T(1,128)} %bitcast.8), calls=%async_computation.1 | async-start | bytes 65536 | tf_op jit(solution)/shard_map/all_to_all | solution.py:68
  27.1 0.8 select_reduce_fusion.2
  27.9 0.9 select_reduce_fusion
  28.8 0.7 convert_bitcast_fusion
  29.7 6.3 gather_fusion
  36.0 8.1 %multiply_convert_fusion = bf16[64,4,128,128]{3,2,1,0:T(8,128)(2,1)} fusion(bf16[64,4,128,128]{3,2,1,0:T(8,128)(2,1)} %gather_fusion, f32[64,128]{1,0:T(8,128)S(1)} %get-tuple-element.7, f32[64,4]{1,0:T(8,128)S(1)} %copy.28, pred[64]{0:T(512)(128)(4,1)S(1)} %get-tuple-element.4, bf16[64,128,128]{2,1,0:T(8,128)(2,1)} %param.9, ...), kind=kOutput, calls=%fused_computation.7 | convolution fusion | flops 1092616192 | bytes 18924608 | tf_op jit(solution)/shard_map/wsij,sjk->swik/dot_general | solution.py:57
  44.1 11.5 %gather_fusion.1 = bf16[128,4,128,128]{3,2,1,0:T(8,128)(2,1)} fusion(bf16[64,4,128,128]{3,2,1,0:T(8,128)(2,1)} %multiply_convert_fusion, s32[1024]{0:T(1024)S(1)} %pad_clamp_fusion.2), kind=kCustom, calls=%fused_computation.1 | custom fusion | bytes 33554944 | tf_op jit(solution)/shard_map/jit(_take)/gather | solution.py:64
  55.6 14.2 %broadcast_select_fusion = bf16[64,2,4,128,128]{4,3,2,1,0:T(8,128)(2,1)} fusion(bf16[64,2,4,128,128]{4,3,2,1,0:T(8,128)(2,1)} %bitcast.42, pred[64,2]{1,0:T(8,128)(4,1)S(1)} %compare_and_fusion.1), kind=kLoop, calls=%fused_computation.9 | loop fusion | flops 8388608 | bytes 33554560 | tf_op jit(solution)/shard_map/jit(_take)/select_n | solution.py:64
  69.8 10.6 %all-to-all-start = ((bf16[64,2,4,128,128]{4,3,2,1,0:T(8,128)(2,1)}), bf16[64,2,4,128,128]{4,3,2,1,0:T(8,128)(2,1)}, u32[]{:S(2)}, u32[]{:S(2)}) async-start(bf16[64,2,4,128,128]{4,3,2,1,0:T(8,128)(2,1)} %broadcast_select_fusion), calls=%async_computation | async-start | bytes 33554432 | tf_op jit(solution)/shard_map/all_to_all | solution.py:67
  80.4 0.2 reduce-scatter.2.cloned.1.call-start
  80.7 0.1 min.18
  81.0 7.9 %gather_fusion.3 = bf16[128,4,128,128]{3,2,1,0:T(8,128)(2,1)} fusion(bf16[4,2,128,128]{3,2,1,0:T(8,128)(2,1)S(1)} %copy-done.1, s32[1024]{0:T(1024)S(1)} %pad_clamp_fusion.1), kind=kCustom, calls=%fused_computation.3 | custom fusion | bytes 33554944 | tf_op jit(solution)/shard_map/jit(_take)/gather | solution.py:73
  89.0 354.0 %all-to-all-done = bf16[64,2,4,128,128]{4,3,2,1,0:T(8,128)(2,1)} async-done(((bf16[64,2,4,128,128]{4,3,2,1,0:T(8,128)(2,1)}), bf16[64,2,4,128,128]{4,3,2,1,0:T(8,128)(2,1)}, u32[]{:S(2)}, u32[]{:S(2)}) %all-to-all-start) | async-done | bytes 16777248 | tf_op jit(solution)/shard_map/all_to_all | solution.py:67
  443.0 16.5 %fusion.8 = f32[64,2,128,128]{3,2,1,0:T(8,128)} fusion(bf16[64,2,4,128,128]{4,3,2,1,0:T(8,128)(2,1)} %all-to-all-done, bf16[4,64,2,128,128]{4,3,0,2,1:T(8,128)(2,1)} %bitcast.43, pred[64,2]{1,0:T(8,128)(4,1)S(1)} %compare_and_fusion), kind=kOutput, calls=%fused_computation.16 | convolution fusion | flops 2155872256 | bytes 41943168 | tf_op jit(solution)/shard_map/ncwij,wnckj->ncik/dot_general | solution.py:75
  459.4 91.8 %reduce-scatter.2.cloned.1.call-done = f32[64,2,32,128]{3,2,1,0:T(8,128)} async-done(((f32[64,2,128,128]{3,2,1,0:T(8,128)}), f32[64,2,32,128]{3,2,1,0:T(8,128)}) %reduce-scatter.2.cloned.1.call-update) | async-done | bytes 2097168 | tf_op jit(solution)/shard_map/reduce_scatter | solution.py:78
  551.2 2.9 convert_element_type.27
  554.1 10.7 %all-to-all-start.2 = ((bf16[64,2,32,128]{3,2,1,0:T(8,128)(2,1)}), bf16[64,2,32,128]{3,2,1,0:T(8,128)(2,1)S(1)}, u32[]{:S(2)}, u32[]{:S(2)}) async-start(bf16[64,2,32,128]{3,2,1,0:T(8,128)(2,1)} %convert_element_type.27), calls=%async_computation.3 | async-start | bytes 2097152 | tf_op jit(solution)/shard_map/all_to_all | solution.py:81
  564.8 28.1 %all-to-all-done.2 = bf16[64,2,32,128]{3,2,1,0:T(8,128)(2,1)S(1)} async-done(((bf16[64,2,32,128]{3,2,1,0:T(8,128)(2,1)}), bf16[64,2,32,128]{3,2,1,0:T(8,128)(2,1)S(1)}, u32[]{:S(2)}, u32[]{:S(2)}) %all-to-all-start.2) | async-done | bytes 1048608 | tf_op jit(solution)/shard_map/all_to_all | solution.py:81
  593.0 1.0 copy-done.2
  594.0 1.9 gather_fusion.4
  595.9 0.1 fusion.33
  596.0 4.7 fusion.17
  600.7 1.0 select_select_fusion
  601.7 74.1 %psum.7 = f32[4]{0:T(128)} all-reduce(f32[4]{0:T(128)S(1)} %fusion.17), channel_id=1, replica_groups=mesh['sec'=64,'op'=4] {'sec','op'}, use_global_device_ids=true, to_apply=%region_6.7 | all-reduce | flops 4 | bytes 32 | tf_op jit(solution)/shard_map/psum | solution.py:89
  (27 shorter events, 0.9 us)
Async XLA Ops:
  7.2 588.8 %copy-start = (bf16[4,64,32,128]{3,2,1,0:T(8,128)(2,1)S(1)}, bf16[4,64,32,128]{3,2,1,0:T(8,128)(2,1)}, u32[]{:S(2)}) copy-start(bf16[4,64,32,128]{3,2,1,0:T(8,128)(2,1)} %param.17) | copy-start | bytes 6291460
  14.0 55.8 %all-to-all-start.1 = ((s32[64,1,2]{2,1,0:T(1,128)}), s32[64,1,2]{2,1,0:T(1,128)S(1)}, u32[]{:S(2)}, u32[]{:S(2)}) async-start(s32[64,1,2]{2,1,0:T(1,128)} %bitcast.8), calls=%async_computation.1 | async-start | bytes 65536 | tf_op jit(solution)/shard_map/all_to_all | solution.py:68
  69.8 11.2 %copy-start.1 = (bf16[4,2,128,128]{3,2,1,0:T(8,128)(2,1)S(1)}, bf16[4,2,128,128]{3,2,1,0:T(8,128)(2,1)}, u32[]{:S(2)}) copy-start(bf16[4,2,128,128]{3,2,1,0:T(8,128)(2,1)} %param.16) | copy-start | bytes 786436
  69.8 373.2 %all-to-all-start = ((bf16[64,2,4,128,128]{4,3,2,1,0:T(8,128)(2,1)}), bf16[64,2,4,128,128]{4,3,2,1,0:T(8,128)(2,1)}, u32[]{:S(2)}, u32[]{:S(2)}) async-start(bf16[64,2,4,128,128]{4,3,2,1,0:T(8,128)(2,1)} %broadcast_select_fusion), calls=%async_computation | async-start | bytes 33554432 | tf_op jit(solution)/shard_map/all_to_all | solution.py:67
  80.4 470.8 %reduce-scatter.2.cloned.1.call-start = ((), (), s32[]{:S(2)}) async-start(), calls=%async_computation.4 | async-start | bytes 10485760 | tf_op jit(solution)/shard_map/reduce_scatter | solution.py:78
  554.1 38.9 %all-to-all-start.2 = ((bf16[64,2,32,128]{3,2,1,0:T(8,128)(2,1)}), bf16[64,2,32,128]{3,2,1,0:T(8,128)(2,1)S(1)}, u32[]{:S(2)}, u32[]{:S(2)}) async-start(bf16[64,2,32,128]{3,2,1,0:T(8,128)(2,1)} %convert_element_type.27), calls=%async_computation.3 | async-start | bytes 2097152 | tf_op jit(solution)/shard_map/all_to_all | solution.py:81
  593.0 1.0 copy-start.2
Sparse Core Ops, SparseCore 0:
  459.6 91.6 reduce-scatter.1
where the time goes:
time: 683 us
  waiting for transfers between devices  474 us (69%)
  blocking collectives  74.1 us (11%)
  starting transfers between devices  34.6 us (5%)
  local copies, waits for them, and re-layouts  32.5 us (5%)
  matrix products  29.2 us (4%)
  other arithmetic  24.1 us (4%)
  between operations  14.2 us (2%)
    all_to_all x1, waiting for transfers between devices, per_device(): lax.all_to_all(outbound, 'sec', split_axis=0, concat_axis=0, tiled=True)  354 us
    reduce_scatter x1, waiting for transfers between devices, per_device(): lax.psum_scatter(partial_value, 'op', scatter_dimension=2, tiled=True)  91.8 us
    psum x1, blocking collectives, per_device(): correlations = lax.psum(local_sum, ('sec', 'op'))  74.1 us
    all_to_all x1, waiting for transfers between devices, per_device(): lax.all_to_all(shares, 'sec', split_axis=0, concat_axis=0, tiled=True)  28.1 us
    dot_general x1, matrix products, per_device(): jnp.einsum('ncwij,wnckj->ncik', tile_set, env_tiles, preferred_element_ty...  16.5 us
    select_n x2, other arithmetic, per_device(): jnp.take(left_part, slot_sector, axis=0)  14.2 us
  transfers between devices with their start and end apart: 4, of which 3 were waited for; matrix products, arithmetic and copies ran while one was open for 7% of the time, Pallas kernels for 0%

commit v1 on v0

v1 whole, which is shorter than its diff:
```python
import jax
import jax.numpy as jnp
from jax import lax
from jax.sharding import PartitionSpec as P


def lookup_small(keys, table):
    table_index = jnp.arange(table.shape[0], dtype=jnp.int32)
    return jnp.sum(jnp.where(keys[:, None] == table_index[None, :], table[None, :], 0), axis=1)


def per_device(
    wavefunction,
    sector_left,
    sector_right,
    left_sizes,
    right_sizes,
    term_mask,
    left_environment,
    right_environment,
    krylov_basis,
):
    holder = lax.axis_index("sec")
    parts = lax.axis_size("op")
    sector_count = wavefunction.shape[0]
    tile_size = wavefunction.shape[1]
    left_per = left_environment.shape[1]
    my_right = lax.dynamic_slice_in_dim(sector_right, holder * sector_count, sector_count)
    everything = lax.all_gather(right_environment, "sec", axis=1, tiled=True)
    lane_index = jnp.arange(tile_size, dtype=jnp.int32)
    left_size = lookup_small(sector_left, left_sizes)
    right_size = lookup_small(my_right, right_sizes)
    rows_inside = lane_index[None, :] < left_size[:, None]
    cols_inside = lane_index[None, :] < right_size[:, None]
    inside = rows_inside[:, :, None] & cols_inside[:, None, :]
    masked_psi = jnp.where(inside, wavefunction, jnp.zeros((), jnp.bfloat16))
    left_index = sector_left - holder * left_per
    left_tiles = jnp.take(left_environment, left_index, axis=1)
    product = jnp.einsum(
        "wsij,sjk->swik", left_tiles, masked_psi, preferred_element_type=jnp.float32
    )
    term_weight = term_mask.T.astype(jnp.float32)[:, :, None, None]
    row_weight = rows_inside.astype(jnp.float32)[:, None, :, None]
    left_part = (product * term_weight * row_weight).astype(jnp.bfloat16)
    env_tiles = jnp.take(everything, my_right, axis=1)
    partial_value = jnp.einsum(
        "swij,wskj->sik", left_part, env_tiles, preferred_element_type=jnp.float32
    ).astype(jnp.bfloat16)
    shares = partial_value.reshape(sector_count, parts, tile_size // parts, tile_size)
    shares = lax.all_to_all(shares, "op", split_axis=1, concat_axis=1, tiled=True)
    result_rows = jnp.sum(shares.astype(jnp.float32), axis=1)
    applied_wave = jnp.where(cols_inside[:, None, :], result_rows, 0.0).astype(jnp.bfloat16)
    local_sum = jnp.einsum(
        "ksij,sij->k", krylov_basis, applied_wave, preferred_element_type=jnp.float32
    )
    correlations = lax.psum(local_sum, ("sec", "op"))
    return (applied_wave, correlations)


def solution(mesh):
    return jax.shard_map(
        per_device,
        mesh=mesh,
        in_specs=(
            P("sec", None, None),
            P("sec"),
            P(),
            P(),
            P(),
            P("op", "sec"),
            P("op", "sec", None, None),
            P("op", "sec", None, None),
            P(None, "sec", "op", None),
        ),
        out_specs=(P("sec", "op", None), P()),
        check_vma=False,
    )
```

time: 683 us -> 255 us (0.37)
  waiting for transfers between devices: 474 us -> 97.9 us
  starting transfers between devices: 34.6 us -> 0.04 us
  blocking collectives: 74.1 us -> 103 us
  other arithmetic: 24.1 us -> 3.99 us
  matrix products: 29.2 us -> 15.7 us
  local copies, waits for them, and re-layouts: 32.5 us -> 19.7 us
    all_to_all x3 -> x0, waiting for transfers between devices: 382 us -> none  [the longest x1 354 us: per_device(): lax.all_to_all(outbound, 'sec', split_axis=0, concat_axis=0, tiled=True)]
    all_gather x0 -> x1, waiting for transfers between devices: none -> 97.2 us  [per_device(): everything = lax.all_gather(right_environment, 'sec', axis=1, tiled=True)]
    reduce_scatter x1 -> x0, waiting for transfers between devices: 91.8 us -> none  [per_device(): lax.psum_scatter(partial_value, 'op', scatter_dimension=2, tiled=True)]
    all_to_all x3 -> x0, starting transfers between devices: 34.3 us -> none  [the longest x1 13 us: per_device(): lax.all_to_all(slot_ids, 'sec', split_axis=0, concat_axis=0, tiled=True)]
    all_to_all x0 -> x1, blocking collectives: none -> 29.7 us  [per_device(): lax.all_to_all(shares, 'op', split_axis=1, concat_axis=1, tiled=True)]
    select_n x8 -> x1, other arithmetic: 15.9 us -> 0.01 us  [per_device(): env_tiles = jnp.take(everything, my_right, axis=1)]
    dot_general x2 -> x1, matrix products: 24.5 us -> 11 us  [per_device(): jnp.einsum('swij,wskj->sik', left_part, env_tiles, preferred_element_type...]
    gather x5 -> x1, local copies, waits for them, and re-layouts: 22.7 us -> 11.3 us  [per_device(): env_tiles = jnp.take(everything, my_right, axis=1)]
  transfers between devices with their start and end apart: 4 -> 1, of which waited for: 3 -> 1; matrix products, arithmetic and copies ran while one was open for 7% -> 4% of each run, Pallas kernels for 0% -> 0%
where the time goes in v1:
time: 255 us; the launch traced here: 254 us
  blocking collectives  103 us (40%)
  waiting for transfers between devices  97.9 us (38%)
  local copies, waits for them, and re-layouts  19.7 us (8%)
  matrix products  15.7 us (6%)
  between operations  14.1 us (6%)
  other arithmetic  3.99 us (2%)
    all_gather x1, waiting for transfers between devices, per_device(): everything = lax.all_gather(right_environment, 'sec', axis=1, tiled=True)  97.2 us
    psum x1, blocking collectives, per_device(): correlations = lax.psum(local_sum, ('sec', 'op'))  73.3 us
    all_to_all x1, blocking collectives, per_device(): lax.all_to_all(shares, 'op', split_axis=1, concat_axis=1, tiled=True)  29.7 us
    gather x1, local copies, waits for them, and re-layouts, per_device(): env_tiles = jnp.take(everything, my_right, axis=1)  11.3 us
    dot_general x1, matrix products, per_device(): jnp.einsum('swij,wskj->sik', left_part, env_tiles, preferred_element_type...  11 us
    gather x1, local copies, waits for them, and re-layouts, per_device(): left_tiles = jnp.take(left_environment, left_index, axis=1)  6.31 us
  transfers between devices with their start and end apart: 1, of which 1 were waited for; matrix products, arithmetic and copies ran while one was open for 4% of the time, Pallas kernels for 0%

profile of v1, /device:TPU:1, one launch (start us, length us, event | category | flops | bytes accessed | tf_op | source)
XLA Modules:
  0.0 254.5 jit_solution(12252454744057345389)
XLA Ops:
  7.2 0.0 copy-start
  7.2 0.0 all-gather.2.cloned.1.call-start
  7.2 0.7 all-gather.2.cloned.1.call-update
  7.9 0.7 convert_bitcast_fusion
  8.6 0.1 copy.14
  8.7 0.7 compare_and_fusion.1
  9.4 0.0 copy-start.1
  9.4 0.0 copy-start.2
  9.4 0.0 copy-start.3
  9.4 6.3 %gather_fusion = bf16[64,4,128,128]{3,2,1,0:T(8,128)(2,1)} fusion(bf16[4,2,128,128]{3,2,1,0:T(8,128)(2,1)} %param.15, s32[1024]{0:T(1024)S(1)} %pad_clamp_fusion.1), kind=kCustom, calls=%fused_computation | custom fusion | bytes 16777472 | tf_op jit(solution)/shard_map/jit(_take)/gather | solution.py:38
  15.7 0.8 compare_and_fusion
  16.5 0.0 copy-done.1
  16.5 0.0 copy-done.2
  16.5 0.2 select_reduce_fusion
  16.7 0.0 copy-done.3
  16.7 0.2 select_reduce_fusion.1
  16.9 0.1 iota_compare_fusion.1
  17.0 97.2 %all-gather.2.cloned.1.call-done = bf16[4,128,128,128]{3,2,1,0:T(8,128)(2,1)} async-done(((bf16[4,2,128,128]{3,2,1,0:T(8,128)(2,1)}), bf16[4,128,128,128]{3,2,1,0:T(8,128)(2,1)}) %all-gather.2.cloned.1.call-update) | async-done | bytes 16777232 | tf_op jit(solution)/shard_map/all_gather | solution.py:29
  114.2 11.3 %gather_fusion.1 = bf16[64,4,128,128]{3,2,1,0:T(8,128)(2,1)} fusion(bf16[4,128,128,128]{3,2,1,0:T(8,128)(2,1)} %all-gather.2.cloned.1.call-done, s32[1024]{0:T(1024)S(1)} %pad_clamp_fusion), kind=kCustom, calls=%fused_computation.1 | custom fusion | bytes 16777472 | tf_op jit(solution)/shard_map/jit(_take)/gather | solution.py:45
  125.5 11.0 %bitcast_convert_fusion = bf16[64,128,128]{2,1,0:T(8,128)(2,1)} fusion(bf16[64,4,128,128]{3,2,1,0:T(8,128)(2,1)} %gather_fusion.1, pred[64]{0:T(512)(128)(4,1)S(1)} %get-tuple-element.4, bf16[64,4,128,128]{3,2,1,0:T(8,128)(2,1)} %gather_fusion, f32[64,128]{1,0:T(8,128)S(1)} %get-tuple-element.7, f32[64,4]{1,0:T(8,128)S(1)} %copy.14, ...), kind=kOutput, calls=%fused_computation.10 | convolution fusion | flops 2171600896 | bytes 21021824 | tf_op jit(solution)/shard_map/swij,wskj->sik/dot_general | solution.py:46
  136.5 2.0 copy.15
  138.5 29.7 %all_to_all.5 = bf16[64,4,32,128]{3,2,0,1:T(8,128)(2,1)S(1)} all-to-all(bf16[64,4,32,128]{3,2,0,1:T(8,128)(2,1)S(1)} %copy.15), channel_id=1, replica_groups=mesh['sec'=64,'op'=4] {'op'}, dimensions={1} | all-to-all | bytes 4194304 | tf_op jit(solution)/shard_map/all_to_all | solution.py:50
  168.2 0.3 convert_reduce_fusion
  168.5 0.2 fusion.32
  168.7 0.0 copy-done
  168.7 4.7 %fusion.21 = f32[4]{0:T(128)S(1)} fusion(bf16[4,64,32,128]{3,2,1,0:T(8,128)(2,1)S(1)} %copy-done, bf16[64,32,128,1]{2,1,0,3:T(8,128)(2,1)S(1)} %fusion.32), kind=kOutput, calls=%fused_computation.20 | convolution fusion | flops 2097152 | bytes 2621456 | tf_op jit(solution)/shard_map/ksij,sij->k/dot_general | solution.py:53
  173.4 1.0 select_convert_fusion
  174.3 73.3 %psum.7 = f32[4]{0:T(128)} all-reduce(f32[4]{0:T(128)S(1)} %fusion.21), channel_id=1, replica_groups=mesh['sec'=64,'op'=4] {'sec','op'}, use_global_device_ids=true, to_apply=%region_3.4 | all-reduce | flops 4 | bytes 32 | tf_op jit(solution)/shard_map/psum | solution.py:56
  (3 shorter events, 0.0 us)
Async XLA Ops:
  7.2 161.5 %copy-start = (bf16[4,64,32,128]{3,2,1,0:T(8,128)(2,1)S(1)}, bf16[4,64,32,128]{3,2,1,0:T(8,128)(2,1)}, u32[]{:S(2)}) copy-start(bf16[4,64,32,128]{3,2,1,0:T(8,128)(2,1)} %param.17) | copy-start | bytes 6291460
  7.2 107.0 %all-gather.2.cloned.1.call-start = ((), (), s32[]{:S(2)}) async-start(), calls=%async_computation.1 | async-start | bytes 17039360 | tf_op jit(solution)/shard_map/all_gather | solution.py:29
  9.4 7.1 %copy-start.1 = (s32[64]{0:T(128)S(1)}, s32[64]{0:T(128)}, u32[]{:S(2)}) copy-start(s32[64]{0:T(128)} %param.10) | copy-start | bytes 772
  9.4 7.1 %copy-start.2 = (s32[128]{0:T(128)S(1)}, s32[128]{0:T(128)}, u32[]{:S(2)}) copy-start(s32[128]{0:T(128)} %param.12) | copy-start | bytes 1540
  9.4 7.3 %copy-start.3 = (s32[128]{0:T(128)S(1)}, s32[128]{0:T(128)}, u32[]{:S(2)}) copy-start(s32[128]{0:T(128)} %param.13) | copy-start | bytes 1540
Sparse Core Ops, SparseCore 0:
  10.8 103.3 all-gather.1

commit v2 on v1

v2 whole, which is shorter than its diff:
```python
import jax
import jax.numpy as jnp
from jax import lax
from jax.experimental import pallas as pl
from jax.experimental.pallas import tpu as pltpu
from jax.sharding import PartitionSpec as P

MESH = pl.DeviceIdType.MESH
NZ, NX, NC, NY = 8, 4, 2, 4
TILE = 128
HALF = 1024
BLOCK = 2 * HALF
SPLIT = {"A": (0, 208), "B": (416, 304)}
GROUP = 4

ORDER = (
    (0, 0), (-1, 0), (0, -1), (0, 1),
    (1, 0), (-2, 0), (-1, -1), (1, -1),
    (1, 1), (0, 2), (-1, 1), (2, 0),
    (-3, 0), (2, -1), (-2, -1), (2, 1),
    (-1, 2), (1, 2), (-2, 1), (3, 0),
    (-3, -1), (3, -1), (3, 1), (-2, 2),
    (2, 2), (-3, 1), (4, 0), (4, -1),
    (-3, 2), (3, 2), (4, 1), (4, 2),
)

PLAN = (
    (("B", 0), ("A", 0),),
    (("B", 1), ("B", 2), ("B", 3), ("B", 4), ("A", 1), ("A", 2), ("A", 3), ("A", 4),),
    (),
    (),
    (("B", 5), ("B", 6), ("B", 10), ("B", 11),),
    (("B", 9), ("A", 5), ("A", 7),),
    (("A", 6), ("A", 8), ("B", 7), ("B", 8),),
    (("A", 9), ("A", 10), ("A", 11),),
    (),
    (),
    (),
    (("B", 14), ("B", 18), ("B", 12), ("B", 19),),
    (("B", 16), ("A", 12), ("A", 13),),
    (("B", 13), ("B", 15), ("A", 14), ("A", 15), ("B", 17),),
    (),
    (("A", 16), ("A", 17), ("B", 23),),
    (),
    (("A", 18), ("A", 19),),
    (("B", 26), ("B", 20), ("B", 25),),
    (),
    (("A", 21), ("A", 20), ("B", 21), ("B", 22), ("A", 22),),
    (("B", 24), ("A", 23),),
    (),
    (("A", 24),),
    (("A", 25), ("A", 26), ("B", 27), ("B", 30),),
    (("A", 27),),
    (("B", 28),),
    (),
    (("A", 28), ("B", 29), ("A", 29), ("A", 30), ("B", 31),),
    (),
    (),
    (("A", 31),),
)

SLOT = {place: index for index, place in enumerate(ORDER)}
BLOCKS = len(ORDER)


def onward(kind, dz, dx):
    out = []
    along_z = kind == "A" or dx == 0
    along_x = kind == "B" or dz == 0
    if along_z:
        if -3 <= dz <= 0:
            out.append(("z+", 2 if dz > -3 else 0, (dz - 1 if dz > -3 else 4, dx)))
        if 0 <= dz <= 3:
            out.append(("z-", 2 if dz < 3 else 1, (dz + 1, dx)))
    if along_x:
        if -1 <= dx <= 0:
            out.append(("x+", 2 if dx == 0 else 0, (dz, -1 if dx == 0 else 2)))
        if 0 <= dx <= 1:
            out.append(("x-", 2 if dx == 0 else 1, (dz, dx + 1)))
    return out


def piece(kind, slot, parts):
    first, rows = SPLIT[kind]
    start = slot * BLOCK + first + (rows if parts == 1 else 0)
    return pl.ds(start, 2 * rows if parts == 2 else rows)


def kernel(
    tab, lenv, rpre, tmask, psi_hbm, kry_hbm,
    applied, corr,
    rbuf, psi, kry, lall, tmall, outb, recvb, sums, gather_z, gather_x, gather_y,
    load_sem, pre_sem, pre_send, side_sem, side_send, a_sem, b_sem, twin_sem, twin_send, link_send,
    out_sem, out_send, own_sem, sum_sem, sum_send,
):
    sec = lax.axis_index("sec")
    y = lax.axis_index("op")
    z = sec // (NX * NC)
    x = (sec // NC) % NX
    core = sec % NC

    def device(dz=0, dx=0, dc=0, dy=0):
        at_z = lax.rem(z + dz + NZ, NZ) if dz else z
        at_x = lax.rem(x + dx + NX, NX) if dx else x
        at_c = 1 - core if dc else core
        at_y = lax.rem(y + dy + NY, NY) if dy else y
        return {"sec": (at_z * NX + at_x) * NC + at_c, "op": at_y}

    def remote(src, dst, send, recv, where):
        return pltpu.make_async_remote_copy(
            src_ref=src, dst_ref=dst, send_sem=send, recv_sem=recv, device_id=where, device_id_type=MESH
        )

    twin = device(dc=1)
    near = {"z+": device(dz=1), "z-": device(dz=-1), "x+": device(dx=1), "x-": device(dx=-1)}
    links = {"z+": 0, "z-": 1, "x+": 2, "x-": 3}

    psi_load = pltpu.make_async_copy(psi_hbm, psi, load_sem.at[0])
    psi_load.start()
    kry_load = pltpu.make_async_copy(kry_hbm, kry, load_sem.at[1])
    kry_load.start()

    barrier = pltpu.get_barrier_semaphore()
    peers = [device(dy=dy, dc=dc) for dy in range(NY) for dc in range(NC) if dy or dc]
    peers += [device(dx=dx) for dx in range(1, NX)] + [device(dz=dz) for dz in range(1, NZ)]
    for peer in peers:
        pl.semaphore_signal(barrier, inc=1, device_id=peer, device_id_type=MESH)
    pl.semaphore_wait(barrier, len(peers))

    for local in range(2):
        target_y = 2 * core + local
        offset = lax.rem(target_y - y + NY, NY)
        for target_core in range(NC):
            mine = (target_y == y) & (core == target_core)
            source = rpre.at[local, target_core]
            landing = rbuf.at[pl.ds(pl.multiple_of(offset * 256, 256), 256)]

            @pl.when(mine)
            def _():
                pltpu.make_async_copy(source, landing, pre_sem.at[offset]).start()

            @pl.when(jnp.logical_not(mine))
            def _():
                remote(
                    source, landing, pre_send, pre_sem.at[offset],
                    {"sec": sec - core + target_core, "op": target_y},
                ).start()

    own_l = pltpu.make_async_copy(lenv, lall.at[0], side_sem.at[0])
    own_t = pltpu.make_async_copy(tmask, tmall.at[0], side_sem.at[NY])
    own_l.start()
    own_t.start()
    sides = []
    for dy in range(1, NY):
        sides.append(remote(tmask, tmall.at[dy], side_send.at[NY + dy], side_sem.at[NY + dy], device(dy=dy)))
        sides.append(remote(lenv, lall.at[dy], side_send.at[dy], side_sem.at[dy], device(dy=dy)))
    for copy in sides:
        copy.start()

    for offset in range(NY):
        part = rbuf.at[pl.ds(offset * 256, 256)]
        pltpu.make_async_copy(part, part, pre_sem.at[offset]).wait()

    def take(kind, slot):
        dz, dx = ORDER[slot]
        whole = rbuf.at[piece(kind, slot, 2)]
        if slot:
            sem = (a_sem if kind == "A" else b_sem).at[slot]
            pltpu.make_async_copy(whole, whole, sem).wait()
        for way, parts, place in onward(kind, dz, dx):
            there = SLOT[place]
            remote(
                rbuf.at[piece(kind, slot, parts)],
                rbuf.at[piece(kind, there, parts)],
                link_send.at[links[way]],
                (a_sem if kind == "A" else b_sem).at[there],
                near[way],
            ).start()

    def half_to_twin(slot):
        remote(
            rbuf.at[pl.ds(slot * BLOCK, HALF)],
            rbuf.at[pl.ds(slot * BLOCK + HALF, HALF)],
            twin_send,
            twin_sem.at[slot],
            twin,
        ).start()

    def branch(index):
        seen = [e for step in PLAN[:index] for e in step]

        def run():
            done = list(seen)
            for kind, slot in PLAN[index]:
                take(kind, slot)
                done.append((kind, slot))
                if ("A", slot) in done and ("B", slot) in done:
                    half_to_twin(slot)

        return run

    branches = [branch(index) for index in range(BLOCKS)]

    def send_group(first):
        for dy in range(NY):
            owner = device(dy=dy)["op"]
            source = outb.at[owner, pl.ds(first, GROUP)]
            landing = recvb.at[pl.ds(dy * BLOCKS + first, GROUP)]
            group = first // GROUP
            if dy == 0:
                pltpu.make_async_copy(source, landing, out_sem.at[0, group]).start()
            else:
                remote(source, landing, out_send, out_sem.at[dy, group], device(dy=dy)).start()

    def product(slot, carry):
        for index, run in enumerate(branches):
            if PLAN[index]:
                pl.when(slot == index)(run)

        @pl.when(slot == 0)
        def _():
            psi_load.wait()
            own_l.wait()
            own_t.wait()
            for copy in sides:
                copy.wait_recv()

        base = pl.multiple_of(slot * BLOCK, BLOCK)
        other = rbuf.at[pl.ds(base + HALF, HALF)]
        pltpu.make_async_copy(other, other, twin_sem.at[slot]).wait()
        s = tab[slot]
        a = tab[BLOCKS + slot]
        block = psi[s]
        total = jnp.zeros((TILE, TILE), jnp.float32)
        for dy in range(NY):
            weights = tmall[dy, pl.ds(s, 1), :]
            for part in range(2):
                left = lall[dy, a, pl.ds(part * 256, 256), :]
                made = jnp.dot(left, block, preferred_element_type=jnp.float32)
                pair = []
                for which in range(2):
                    lane = part * 2 + which
                    weight = jnp.broadcast_to(weights[:, lane : lane + 1], (TILE, TILE))
                    pair.append((made[which * TILE : (which + 1) * TILE] * weight).astype(jnp.bfloat16))
                start = pl.multiple_of(base + part * HALF + dy * 256, 256)
                first = rbuf[pl.ds(start, TILE), :]
                second = rbuf[pl.ds(start + TILE, TILE), :]
                total = total + lax.dot_general(
                    jnp.concatenate(pair, axis=1),
                    jnp.concatenate([first, second], axis=1),
                    (((1,), (1,)), ((), ())),
                    preferred_element_type=jnp.float32,
                )
        result = total.astype(jnp.bfloat16)
        rows = TILE // NY
        for owner in range(NY):
            outb[owner, slot] = result[owner * rows : (owner + 1) * rows]

        @pl.when(lax.rem(slot, GROUP) == GROUP - 1)
        def _():
            send_group(slot - (GROUP - 1))

        return carry

    lax.fori_loop(0, BLOCKS, product, 0)

    kry_load.wait()
    for dy in range(NY):
        for group in range(BLOCKS // GROUP):
            landing = recvb.at[pl.ds(dy * BLOCKS + group * GROUP, GROUP)]
            pltpu.make_async_copy(landing, landing, out_sem.at[dy, group]).wait()

    vectors = kry.shape[0]

    def collect(s, accs):
        rows = recvb[tab[2 * BLOCKS + s]]
        applied[s] = rows
        wide = rows.astype(jnp.float32)
        return tuple(accs[k] + kry[k, s].astype(jnp.float32) * wide for k in range(vectors))

    zero = jnp.zeros((TILE // NY, TILE), jnp.float32)
    accs = lax.fori_loop(0, psi.shape[0], collect, (zero,) * vectors)
    flat = [jnp.sum(acc, axis=0, keepdims=True) for acc in accs]
    flat += [jnp.zeros((8 - vectors, TILE), jnp.float32)]
    held = jnp.concatenate(flat, axis=0)

    stages = (
        (gather_y, y * NC + core, [(device(dy=dy, dc=dc)) for dy in range(NY) for dc in range(NC) if dy or dc]),
        (gather_x, x, [device(dx=dx) for dx in range(1, NX)]),
        (gather_z, z, [device(dz=dz) for dz in range(1, NZ)]),
    )
    for stage, (gather, place, targets) in enumerate(stages):
        sums[stage] = held
        gather[place] = held
        for target in targets:
            remote(sums.at[stage], gather.at[place], sum_send.at[stage], sum_sem.at[stage], target).start()
        most = gather.at[pl.ds(0, len(targets))]
        pltpu.make_async_copy(most, most, sum_sem.at[stage]).wait()
        held = jnp.sum(gather[...], axis=0)
    corr[...] = jnp.broadcast_to(jnp.sum(held, axis=1, keepdims=True), corr.shape)

    def sent(ref, sem):
        pltpu.make_async_copy(ref, ref, sem).wait()

    totals = dict.fromkeys(links, 0)
    for kind in ("A", "B"):
        for dz, dx in ORDER:
            for way, parts, _ in onward(kind, dz, dx):
                totals[way] += SPLIT[kind][1] * (2 if parts == 2 else 1)
    for way, rows in totals.items():
        sent(rbuf.at[pl.ds(0, rows)], link_send.at[links[way]])
    sent(rbuf.at[pl.ds(0, BLOCKS * HALF)], twin_send)
    for copy in sides:
        copy.wait_send()
    sent(recvb.at[pl.ds(0, (NY - 1) * BLOCKS)], out_send)
    for stage, (gather, place, targets) in enumerate(stages):
        sent(gather.at[pl.ds(0, len(targets))], sum_send.at[stage])
    any_mine = (y // 2) == core

    @pl.when(any_mine)
    def _():
        sent(rbuf.at[pl.ds(0, 3 * 256)], pre_send)

    @pl.when(jnp.logical_not(any_mine))
    def _():
        sent(rbuf.at[pl.ds(0, 4 * 256)], pre_send)


def per_device(
    wavefunction,
    sector_left,
    sector_right,
    left_sizes,
    right_sizes,
    term_mask,
    left_environment,
    right_environment,
    krylov_basis,
):
    sec = lax.axis_index("sec")
    y = lax.axis_index("op")
    z, x, core = sec // (NX * NC), (sec // NC) % NX, sec % NC
    sectors = wavefunction.shape[0]
    terms, left_per = left_environment.shape[:2]
    right_per = right_environment.shape[1]
    lane = jnp.arange(TILE, dtype=jnp.int32)

    places = jnp.array(ORDER, dtype=jnp.int32)
    chips = ((z + places[:, 0] + NZ) % NZ) * NX + (x + places[:, 1] + NX) % NX
    numbers = chips * NY + y
    my_right = lax.dynamic_slice_in_dim(sector_right, sec * sectors, sectors)
    match = numbers[:, None] == my_right[None, :]
    sector_at = jnp.arange(sectors, dtype=jnp.int32)
    s_of = jnp.sum(jnp.where(match, sector_at[None, :], 0), axis=1)
    a_of = jnp.sum(jnp.where(match, (sector_left - sec * left_per)[None, :], 0), axis=1)
    same_chip = (my_right // NY)[:, None] == chips[None, :]
    use_of = jnp.sum(jnp.where(same_chip, jnp.arange(BLOCKS, dtype=jnp.int32)[None, :], 0), axis=1)
    slot_of = ((y - my_right % NY + NY) % NY) * BLOCKS + use_of
    tab = jnp.concatenate([s_of, a_of, slot_of]).astype(jnp.int32)

    left_size = lax.dynamic_slice_in_dim(left_sizes, sec * left_per, left_per)
    right_size = lax.dynamic_slice_in_dim(right_sizes, sec * right_per, right_per)
    left_in = lane[None, :] < left_size[:, None]
    right_in = lane[None, :] < right_size[:, None]
    none = jnp.zeros((), jnp.bfloat16)
    left = jnp.where((left_in[:, :, None] & left_in[:, None, :])[None], left_environment, none)
    right = jnp.where((right_in[:, :, None] & right_in[:, None, :])[None], right_environment, none)
    halves = left.reshape(2, 2, left_per, TILE, TILE)
    halves = jnp.where(core == 0, halves, halves[::-1])
    lenv = halves.reshape(terms, left_per, TILE, TILE).transpose(1, 0, 2, 3).reshape(left_per, terms * TILE, TILE)
    rpre = right.reshape(2, 2, right_per, TILE, TILE).transpose(2, 0, 1, 3, 4).reshape(right_per, 2, 2 * TILE, TILE)
    mask = term_mask.reshape(2, 2, sectors)
    mask = jnp.where(core == 0, mask, mask[::-1]).reshape(terms, sectors)
    tmask = jnp.pad(mask.T.astype(jnp.float32), ((0, 0), (0, TILE - terms)))

    rows = TILE // NY
    vectors = krylov_basis.shape[0]
    dma = pltpu.SemaphoreType.DMA
    vmem = pl.BlockSpec(memory_space=pltpu.VMEM)
    anywhere = pl.BlockSpec(memory_space=pl.ANY)
    applied, corr = pl.pallas_call(
        kernel,
        name="bond_apply",
        out_shape=(
            jax.ShapeDtypeStruct((sectors, rows, TILE), jnp.bfloat16),
            jax.ShapeDtypeStruct((8, TILE), jnp.float32),
        ),
        in_specs=[pl.BlockSpec(memory_space=pltpu.SMEM), vmem, vmem, vmem, anywhere, anywhere],
        out_specs=(vmem, vmem),
        scratch_shapes=[
            pltpu.VMEM((BLOCKS * BLOCK, TILE), jnp.bfloat16),
            pltpu.VMEM((sectors, TILE, TILE), jnp.bfloat16),
            pltpu.VMEM((vectors, sectors, rows, TILE), jnp.bfloat16),
            pltpu.VMEM((NY, left_per, terms * TILE, TILE), jnp.bfloat16),
            pltpu.VMEM((NY, sectors, TILE), jnp.float32),
            pltpu.VMEM((NY, BLOCKS, rows, TILE), jnp.bfloat16),
            pltpu.VMEM((NY * BLOCKS, rows, TILE), jnp.bfloat16),
            pltpu.VMEM((3, 8, TILE), jnp.float32),
            pltpu.VMEM((NZ, 8, TILE), jnp.float32),
            pltpu.VMEM((NX, 8, TILE), jnp.float32),
            pltpu.VMEM((NY * NC, 8, TILE), jnp.float32),
            dma((2,)),
            dma((NY,)),
            dma,
            dma((2 * NY,)),
            dma((2 * NY,)),
            dma((BLOCKS,)),
            dma((BLOCKS,)),
            dma((BLOCKS,)),
            dma,
            dma((4,)),
            dma((NY, BLOCKS // GROUP)),
            dma,
            dma,
            dma((3,)),
            dma((3,)),
        ],
        compiler_params=pltpu.CompilerParams(
            collective_id=0, has_side_effects=True, vmem_limit_bytes=48 * 1024 * 1024
        ),
    )(tab, lenv, rpre, tmask, wavefunction, krylov_basis)
    return applied, corr[:vectors, 0]


def solution(mesh):
    return jax.shard_map(
        per_device,
        mesh=mesh,
        in_specs=(
            P("sec", None, None),
            P("sec"),
            P(),
            P(),
            P(),
            P("op", "sec"),
            P("op", "sec", None, None),
            P("op", "sec", None, None),
            P(None, "sec", "op", None),
        ),
        out_specs=(P("sec", "op", None), P()),
        check_vma=False,
    )
```

time: 255 us -> 107 us (0.42)
  blocking collectives: 103 us -> 0 us
  waiting for transfers between devices: 97.9 us -> 0 us
  Pallas kernels: 0 us -> 95.7 us
  matrix products: 15.7 us -> 0 us
  local copies, waits for them, and re-layouts: 19.7 us -> 4.75 us
  between operations: 14.1 us -> 0.77 us
    all_gather x1 -> x0, waiting for transfers between devices: 97.2 us -> none  [per_device(): everything = lax.all_gather(right_environment, 'sec', axis=1, tiled=True)]
    pallas_call x0 -> x1, Pallas kernels: none -> 95.7 us  [per_device(): pl.pallas_call(kernel, name='bond_apply', out_shape=(jax.ShapeDtypeStruct...]
    psum x1 -> x0, blocking collectives: 73.3 us -> none  [per_device(): correlations = lax.psum(local_sum, ('sec', 'op'))]
    all_to_all x1 -> x0, blocking collectives: 29.7 us -> none  [per_device(): lax.all_to_all(shares, 'op', split_axis=1, concat_axis=1, tiled=True)]
    gather x2 -> x0, local copies, waits for them, and re-layouts: 17.6 us -> none  [the longest x1 11.3 us: per_device(): env_tiles = jnp.take(everything, my_right, axis=1)]
    dot_general x2 -> x0, matrix products: 15.7 us -> none  [the longest x1 11 us: per_device(): jnp.einsum('swij,wskj->sik', left_part, env_tiles, preferred_element_type...]
    select_n x1 -> x4, other arithmetic: 0.01 us -> 2.78 us  [the longest x1 0.98 us: per_device(): jnp.where((right_in[:, :, None] & right_in[:, None, :])[None], right_envi...]
  transfers between devices with their start and end apart: 1 -> 0, of which waited for: 1 -> 0; matrix products, arithmetic and copies ran while one was open for 4% -> 0% of each run, Pallas kernels for 0% -> 0%
where the time goes in v2:
time: 107 us
  Pallas kernels  95.7 us (89%)
  other arithmetic  5.63 us (5%)
  local copies, waits for them, and re-layouts  4.75 us (4%)
    pallas_call x1, Pallas kernels, per_device(): pl.pallas_call(kernel, name='bond_apply', out_shape=(jax.ShapeDtypeStruct...  95.7 us
    unnamed x5, local copies, waits for them, and re-layouts  2.38 us

profile of v2, /device:TPU:1, one launch (start us, length us, event | category | flops | bytes accessed | tf_op | source)
XLA Modules:
  0.0 106.8 jit_solution(13552147937571862877)
XLA Ops:
  0.6 0.0 copy-start
  0.7 0.9 dynamic_slice.10
  1.6 0.7 dynamic_slice.11
  2.3 0.1 iota_compare_fusion
  2.4 0.1 iota_compare_fusion.1
  2.4 0.7 fusion.4
  3.1 0.7 add_bitcast_fusion
  3.8 0.8 and_select_fusion.2
  4.6 0.1 select_reduce_fusion
  4.7 0.2 fusion
  4.9 0.1 pad_add_fusion.tab
  5.0 0.8 fusion.2
  5.7 0.1 copy.21
  5.8 0.1 broadcast_and_fusion.1
  5.9 0.1 broadcast_and_fusion
  6.0 1.0 broadcast_select_fusion
  7.1 1.0 broadcast_select_fusion.1
  8.0 0.1 reverse_select_fusion
  8.1 0.0 copy-done
  8.1 0.0 copy-start.1
  8.1 1.6 %copy-done.1 = bf16[4,64,32,128]{3,2,1,0:T(8,128)(2,1)S(1)} copy-done((bf16[4,64,32,128]{3,2,1,0:T(8,128)(2,1)S(1)}, bf16[4,64,32,128]{3,2,1,0:T(8,128)(2,1)}, u32[]{:S(2)}) %copy-start.1) | copy-done | bytes 2097176
  9.7 95.7 %bond_apply.1 = (bf16[64,32,128]{2,1,0:T(8,128)(2,1)S(1)}, f32[8,128]{1,0:T(8,128)S(1)}) custom-call(s32[128]{0:T(128)S(1)} %pad_add_fusion.tab, bf16[2,512,128]{2,1,0:T(8,128)(2,1)S(1)} %bitcast.20, bf16[2,2,256,128]{3,2,1,0:T(8,128)(2,1)S(1)} %bitcast.19, f32[64,128]{1,0:T(8,128)S(1)} %pad.4.tmask, bf16[64,128,128]{2,1,0:T(8,128)(2,1)S(1)} %copy-done, ...), custom_call_target="tpu_custom_call" | custom-call | tf_op jit(solution)/shard_map/bond_apply/pallas_call | solution.py:381
  105.4 0.6 slice_reduce_fusion
  106.0 0.8 copy.23
  (4 shorter events, 0.1 us)
Async XLA Ops:
  0.6 7.5 %copy-start = (bf16[64,128,128]{2,1,0:T(8,128)(2,1)S(1)}, bf16[64,128,128]{2,1,0:T(8,128)(2,1)}, u32[]{:S(2)}) copy-start(bf16[64,128,128]{2,1,0:T(8,128)(2,1)} %psi_hbm.1) | copy-start | bytes 6291460
  8.1 1.6 %copy-start.1 = (bf16[4,64,32,128]{3,2,1,0:T(8,128)(2,1)S(1)}, bf16[4,64,32,128]{3,2,1,0:T(8,128)(2,1)}, u32[]{:S(2)}) copy-start(bf16[4,64,32,128]{3,2,1,0:T(8,128)(2,1)} %kry_hbm.1) | copy-start | bytes 6291460

commit v3 on v2

--- a/solution.py
+++ b/solution.py
@@ -14,49 +14,49 @@
 GROUP = 4
 
 ORDER = (
-    (0, 0), (-1, 0), (0, -1), (0, 1),
+    (-1, 0), (0, -1), (0, 0), (0, 1),
     (1, 0), (-2, 0), (-1, -1), (1, -1),
     (1, 1), (0, 2), (-1, 1), (2, 0),
     (-3, 0), (2, -1), (-2, -1), (2, 1),
     (-1, 2), (1, 2), (-2, 1), (3, 0),
     (-3, -1), (3, -1), (3, 1), (-2, 2),
     (2, 2), (-3, 1), (4, 0), (4, -1),
-    (-3, 2), (3, 2), (4, 1), (4, 2),
+    (4, 1), (-3, 2), (3, 2), (4, 2),
 )
 
 PLAN = (
-    (("B", 0), ("A", 0),),
-    (("B", 1), ("B", 2), ("B", 3), ("B", 4), ("A", 1), ("A", 2), ("A", 3), ("A", 4),),
-    (),
-    (),
-    (("B", 5), ("B", 6), ("B", 10), ("B", 11),),
-    (("B", 9), ("A", 5), ("A", 7),),
-    (("A", 6), ("A", 8), ("B", 7), ("B", 8),),
-    (("A", 9), ("A", 10), ("A", 11),),
-    (),
-    (),
-    (),
-    (("B", 14), ("B", 18), ("B", 12), ("B", 19),),
-    (("B", 16), ("A", 12), ("A", 13),),
-    (("B", 13), ("B", 15), ("A", 14), ("A", 15), ("B", 17),),
-    (),
-    (("A", 16), ("A", 17), ("B", 23),),
+    (("B", 2), ("A", 2), ("B", 0), ("B", 1), ("B", 3), ("B", 4), ("A", 0), ("A", 1), ("A", 3), ("A", 4), ("B", 5), ("B", 6), ("B", 10), ("B", 11), ("B", 9), ("A", 5), ("A", 7),),
+    (),
+    (("A", 6), ("A", 8),),
+    (("B", 7), ("B", 8),),
+    (("A", 9),),
+    (("A", 10), ("A", 11),),
+    (),
+    (),
+    (("B", 14), ("B", 18),),
+    (("B", 12), ("B", 19),),
+    (("B", 16),),
+    (("A", 12), ("A", 13),),
+    (("B", 13), ("B", 15), ("A", 14), ("A", 15),),
+    (("B", 17), ("A", 16), ("A", 17),),
+    (("B", 23),),
     (),
     (("A", 18), ("A", 19),),
+    (),
     (("B", 26), ("B", 20), ("B", 25),),
-    (),
-    (("A", 21), ("A", 20), ("B", 21), ("B", 22), ("A", 22),),
-    (("B", 24), ("A", 23),),
-    (),
+    (("A", 21),),
+    (("A", 20), ("B", 21), ("B", 22), ("A", 22), ("B", 24), ("A", 23),),
     (("A", 24),),
-    (("A", 25), ("A", 26), ("B", 27), ("B", 30),),
-    (("A", 27),),
-    (("B", 28),),
-    (),
-    (("A", 28), ("B", 29), ("A", 29), ("A", 30), ("B", 31),),
-    (),
+    (("A", 25), ("A", 26),),
+    (("B", 27), ("B", 28), ("A", 27),),
+    (("B", 29),),
+    (),
+    (("A", 29), ("B", 30),),
+    (("A", 30), ("A", 28),),
+    (("B", 31),),
     (),
     (("A", 31),),
+    (),
 )
 
 SLOT = {place: index for index, place in enumerate(ORDER)}
@@ -87,9 +87,9 @@
 
 
 def kernel(
-    tab, lenv, rpre, tmask, psi_hbm, kry_hbm,
+    places, sector_left, left_sizes, right_sizes, my_right, right_rows, tmask, left_hbm, right_hbm, psi_hbm, kry_hbm,
     applied, corr,
-    rbuf, psi, kry, lall, tmall, outb, recvb, sums, gather_z, gather_x, gather_y,
+    rbuf, psi, kry, lall, tmall, flat_mask, turned_mask, outb, recvb, sums, gather_z, gather_x, gather_y,
     load_sem, pre_sem, pre_send, side_sem, side_send, a_sem, b_sem, twin_sem, twin_send, link_send,
     out_sem, out_send, own_sem, sum_sem, sum_send,
 ):
@@ -111,6 +111,7 @@
             src_ref=src, dst_ref=dst, send_sem=send, recv_sem=recv, device_id=where, device_id_type=MESH
         )
 
+    terms, left_per = left_hbm.shape[:2]
     twin = device(dc=1)
     near = {"z+": device(dz=1), "z-": device(dz=-1), "x+": device(dx=1), "x-": device(dx=-1)}
     links = {"z+": 0, "z-": 1, "x+": 2, "x-": 3}
@@ -130,10 +131,11 @@
     for local in range(2):
         target_y = 2 * core + local
         offset = lax.rem(target_y - y + NY, NY)
-        for target_core in range(NC):
+        for target_core, which in ((0, 0), (0, 1), (1, 0), (1, 1)):
             mine = (target_y == y) & (core == target_core)
-            source = rpre.at[local, target_core]
-            landing = rbuf.at[pl.ds(pl.multiple_of(offset * 256, 256), 256)]
+            source = right_hbm.at[2 * target_core + which, local]
+            start = SLOT[0, 0] * BLOCK + which * TILE + offset * 256
+            landing = rbuf.at[pl.ds(pl.multiple_of(start, TILE), TILE)]
 
             @pl.when(mine)
             def _():
@@ -146,25 +148,25 @@
                     {"sec": sec - core + target_core, "op": target_y},
                 ).start()
 
-    own_l = pltpu.make_async_copy(lenv, lall.at[0], side_sem.at[0])
+    own_l = pltpu.make_async_copy(left_hbm, lall.at[0], side_sem.at[0])
     own_t = pltpu.make_async_copy(tmask, tmall.at[0], side_sem.at[NY])
     own_l.start()
     own_t.start()
     sides = []
     for dy in range(1, NY):
         sides.append(remote(tmask, tmall.at[dy], side_send.at[NY + dy], side_sem.at[NY + dy], device(dy=dy)))
-        sides.append(remote(lenv, lall.at[dy], side_send.at[dy], side_sem.at[dy], device(dy=dy)))
+        sides.append(remote(left_hbm, lall.at[dy], side_send.at[dy], side_sem.at[dy], device(dy=dy)))
     for copy in sides:
         copy.start()
 
     for offset in range(NY):
-        part = rbuf.at[pl.ds(offset * 256, 256)]
+        part = rbuf.at[pl.ds(SLOT[0, 0] * BLOCK + offset * 256, 256)]
         pltpu.make_async_copy(part, part, pre_sem.at[offset]).wait()
 
     def take(kind, slot):
         dz, dx = ORDER[slot]
         whole = rbuf.at[piece(kind, slot, 2)]
-        if slot:
+        if dz or dx:
             sem = (a_sem if kind == "A" else b_sem).at[slot]
             pltpu.make_async_copy(whole, whole, sem).wait()
         for way, parts, place in onward(kind, dz, dx):
@@ -212,37 +214,56 @@
             else:
                 remote(source, landing, out_send, out_sem.at[dy, group], device(dy=dy)).start()
 
+    def prepare():
+        psi_load.wait()
+        own_l.wait()
+        own_t.wait()
+        for copy in sides:
+            copy.wait_recv()
+        down = lax.broadcasted_iota(jnp.int32, (TILE, TILE), 0)
+        across = lax.broadcasted_iota(jnp.int32, (TILE, TILE), 1)
+        for a in range(left_per):
+            size = left_sizes[sec * left_per + a]
+            inside = jnp.where((down < size) & (across < size), 1.0, 0.0).astype(jnp.bfloat16)
+            for dy in range(NY):
+                for term in range(terms):
+                    lall[dy, term, a] = lall[dy, term, a] * inside
+        flat_mask[...] = jnp.zeros_like(flat_mask)
+        for dy in range(NY):
+            flat_mask[dy * terms : (dy + 1) * terms, 0 : tmall.shape[2]] = tmall[dy].astype(jnp.float32)
+        turned_mask[...] = flat_mask[...].T
+
     def product(slot, carry):
         for index, run in enumerate(branches):
             if PLAN[index]:
                 pl.when(slot == index)(run)
 
-        @pl.when(slot == 0)
-        def _():
-            psi_load.wait()
-            own_l.wait()
-            own_t.wait()
-            for copy in sides:
-                copy.wait_recv()
-
+        pl.when(slot == 0)(prepare)
         base = pl.multiple_of(slot * BLOCK, BLOCK)
         other = rbuf.at[pl.ds(base + HALF, HALF)]
         pltpu.make_async_copy(other, other, twin_sem.at[slot]).wait()
-        s = tab[slot]
-        a = tab[BLOCKS + slot]
-        block = psi[s]
+        chip = lax.rem(z + places[BLOCKS + slot], NZ) * NX + lax.rem(x + places[2 * BLOCKS + slot], NX)
+        number = chip * NY + y
+        row = right_rows[pl.ds(sec // 2, 1), :]
+        place = lax.broadcasted_iota(jnp.int32, (1, TILE), 1) - core * (TILE // 2)
+        match = (row == number) & (place >= 0) & (place < TILE // 2)
+        s = jnp.max(jnp.where(match, place, 0))
+        a = lax.rem(sector_left[s], left_per)
+        col_in = lax.broadcasted_iota(jnp.int32, (1, TILE), 1) < right_sizes[number]
+        block = psi[s] * jnp.where(col_in, 1.0, 0.0).astype(jnp.bfloat16)
+        weights = turned_mask[pl.ds(s, 1), :]
         total = jnp.zeros((TILE, TILE), jnp.float32)
         for dy in range(NY):
-            weights = tmall[dy, pl.ds(s, 1), :]
             for part in range(2):
-                left = lall[dy, a, pl.ds(part * 256, 256), :]
+                left = jnp.concatenate([lall[dy, 2 * part, a], lall[dy, 2 * part + 1, a]], axis=0)
                 made = jnp.dot(left, block, preferred_element_type=jnp.float32)
                 pair = []
                 for which in range(2):
-                    lane = part * 2 + which
+                    lane = dy * terms + part * 2 + which
                     weight = jnp.broadcast_to(weights[:, lane : lane + 1], (TILE, TILE))
                     pair.append((made[which * TILE : (which + 1) * TILE] * weight).astype(jnp.bfloat16))
-                start = pl.multiple_of(base + part * HALF + dy * 256, 256)
+                away = HALF * (core if part == 0 else 1 - core)
+                start = pl.multiple_of(base + away + dy * 256, 256)
                 first = rbuf[pl.ds(start, TILE), :]
                 second = rbuf[pl.ds(start + TILE, TILE), :]
                 total = total + lax.dot_general(
@@ -251,6 +272,7 @@
                     (((1,), (1,)), ((), ())),
                     preferred_element_type=jnp.float32,
                 )
+        total = jnp.where(col_in, total, 0.0)
         result = total.astype(jnp.bfloat16)
         rows = TILE // NY
         for owner in range(NY):
@@ -273,13 +295,18 @@
     vectors = kry.shape[0]
 
     def collect(s, accs):
-        rows = recvb[tab[2 * BLOCKS + s]]
+        number = my_right[sec * psi.shape[0] + s]
+        chip = number // NY
+        away_z = lax.rem(chip // NX - z + NZ, NZ)
+        away_x = lax.rem(chip % NX - x + NX, NX)
+        plane = lax.rem(y - number % NY + NY, NY)
+        rows = recvb[plane * BLOCKS + places[away_z * NX + away_x]]
         applied[s] = rows
         wide = rows.astype(jnp.float32)
         return tuple(accs[k] + kry[k, s].astype(jnp.float32) * wide for k in range(vectors))
 
     zero = jnp.zeros((TILE // NY, TILE), jnp.float32)
-    accs = lax.fori_loop(0, psi.shape[0], collect, (zero,) * vectors)
+    accs = lax.fori_loop(0, psi.shape[0], collect, (zero,) * vectors, unroll=4)
     flat = [jnp.sum(acc, axis=0, keepdims=True) for acc in accs]
     flat += [jnp.zeros((8 - vectors, TILE), jnp.float32)]
     held = jnp.concatenate(flat, axis=0)
@@ -337,46 +364,17 @@
     right_environment,
     krylov_basis,
 ):
-    sec = lax.axis_index("sec")
-    y = lax.axis_index("op")
-    z, x, core = sec // (NX * NC), (sec // NC) % NX, sec % NC
     sectors = wavefunction.shape[0]
     terms, left_per = left_environment.shape[:2]
-    right_per = right_environment.shape[1]
-    lane = jnp.arange(TILE, dtype=jnp.int32)
-
-    places = jnp.array(ORDER, dtype=jnp.int32)
-    chips = ((z + places[:, 0] + NZ) % NZ) * NX + (x + places[:, 1] + NX) % NX
-    numbers = chips * NY + y
-    my_right = lax.dynamic_slice_in_dim(sector_right, sec * sectors, sectors)
-    match = numbers[:, None] == my_right[None, :]
-    sector_at = jnp.arange(sectors, dtype=jnp.int32)
-    s_of = jnp.sum(jnp.where(match, sector_at[None, :], 0), axis=1)
-    a_of = jnp.sum(jnp.where(match, (sector_left - sec * left_per)[None, :], 0), axis=1)
-    same_chip = (my_right // NY)[:, None] == chips[None, :]
-    use_of = jnp.sum(jnp.where(same_chip, jnp.arange(BLOCKS, dtype=jnp.int32)[None, :], 0), axis=1)
-    slot_of = ((y - my_right % NY + NY) % NY) * BLOCKS + use_of
-    tab = jnp.concatenate([s_of, a_of, slot_of]).astype(jnp.int32)
-
-    left_size = lax.dynamic_slice_in_dim(left_sizes, sec * left_per, left_per)
-    right_size = lax.dynamic_slice_in_dim(right_sizes, sec * right_per, right_per)
-    left_in = lane[None, :] < left_size[:, None]
-    right_in = lane[None, :] < right_size[:, None]
-    none = jnp.zeros((), jnp.bfloat16)
-    left = jnp.where((left_in[:, :, None] & left_in[:, None, :])[None], left_environment, none)
-    right = jnp.where((right_in[:, :, None] & right_in[:, None, :])[None], right_environment, none)
-    halves = left.reshape(2, 2, left_per, TILE, TILE)
-    halves = jnp.where(core == 0, halves, halves[::-1])
-    lenv = halves.reshape(terms, left_per, TILE, TILE).transpose(1, 0, 2, 3).reshape(left_per, terms * TILE, TILE)
-    rpre = right.reshape(2, 2, right_per, TILE, TILE).transpose(2, 0, 1, 3, 4).reshape(right_per, 2, 2 * TILE, TILE)
-    mask = term_mask.reshape(2, 2, sectors)
-    mask = jnp.where(core == 0, mask, mask[::-1]).reshape(terms, sectors)
-    tmask = jnp.pad(mask.T.astype(jnp.float32), ((0, 0), (0, TILE - terms)))
+    by_place = [SLOT[(dz + 3) % NZ - 3, (dx + 1) % NX - 1] for dz in range(NZ) for dx in range(NX)]
+    places = by_place + [dz % NZ for dz, _ in ORDER] + [dx % NX for _, dx in ORDER]
+    places = jnp.array(places, dtype=jnp.int32)
 
     rows = TILE // NY
     vectors = krylov_basis.shape[0]
     dma = pltpu.SemaphoreType.DMA
     vmem = pl.BlockSpec(memory_space=pltpu.VMEM)
+    smem = pl.BlockSpec(memory_space=pltpu.SMEM)
     anywhere = pl.BlockSpec(memory_space=pl.ANY)
     applied, corr = pl.pallas_call(
         kernel,
@@ -385,14 +383,16 @@
             jax.ShapeDtypeStruct((sectors, rows, TILE), jnp.bfloat16),
             jax.ShapeDtypeStruct((8, TILE), jnp.float32),
         ),
-        in_specs=[pl.BlockSpec(memory_space=pltpu.SMEM), vmem, vmem, vmem, anywhere, anywhere],
+        in_specs=[smem] * 5 + [vmem] * 2 + [anywhere] * 4,
         out_specs=(vmem, vmem),
         scratch_shapes=[
             pltpu.VMEM((BLOCKS * BLOCK, TILE), jnp.bfloat16),
             pltpu.VMEM((sectors, TILE, TILE), jnp.bfloat16),
             pltpu.VMEM((vectors, sectors, rows, TILE), jnp.bfloat16),
-            pltpu.VMEM((NY, left_per, terms * TILE, TILE), jnp.bfloat16),
-            pltpu.VMEM((NY, sectors, TILE), jnp.float32),
+            pltpu.VMEM((NY, terms, left_per, TILE, TILE), jnp.bfloat16),
+            pltpu.VMEM((NY, terms, sectors), jnp.int32),
+            pltpu.VMEM((TILE, TILE), jnp.float32),
+            pltpu.VMEM((TILE, TILE), jnp.float32),
             pltpu.VMEM((NY, BLOCKS, rows, TILE), jnp.bfloat16),
             pltpu.VMEM((NY * BLOCKS, rows, TILE), jnp.bfloat16),
             pltpu.VMEM((3, 8, TILE), jnp.float32),
@@ -416,9 +416,21 @@
             dma((3,)),
         ],
         compiler_params=pltpu.CompilerParams(
-            collective_id=0, has_side_effects=True, vmem_limit_bytes=48 * 1024 * 1024
+            collective_id=0, has_side_effects=True, vmem_limit_bytes=60 * 1024 * 1024
         ),
-    )(tab, lenv, rpre, tmask, wavefunction, krylov_basis)
+    )(
+        places,
+        sector_left,
+        left_sizes,
+        right_sizes,
+        sector_right,
+        sector_right.reshape(-1, TILE),
+        term_mask,
+        left_environment,
+        right_environment,
+        wavefunction,
+        krylov_basis,
+    )
     return applied, corr[:vectors, 0]
 
 

time: 107 us -> 107 us (level)
  Pallas kernels: 95.7 us -> 103 us
  other arithmetic: 5.63 us -> 0 us
  local copies, waits for them, and re-layouts: 4.75 us -> 3.18 us
    pallas_call x1, Pallas kernels: 95.7 us -> 103 us  [per_device(): pl.pallas_call(kernel, name='bond_apply', out_shape=(jax.ShapeDtypeStruct...]
    select_n x4 -> x0, other arithmetic: 2.78 us -> none  [the longest x1 0.98 us: per_device(): jnp.where((right_in[:, :, None] & right_in[:, None, :])[None], right_envi...]
    dynamic_slice x2 -> x0, local copies, waits for them, and re-layouts: 1.6 us -> none  [the longest x1 0.87 us: per_device(): left_size = lax.dynamic_slice_in_dim(left_sizes, sec * left_per, left_per)]
    unnamed x5 -> x1, local copies, waits for them, and re-layouts: 2.38 us -> 1.87 us
where the time goes in v3:
time: 107 us; the launch traced here: 106 us
  Pallas kernels  103 us (96%)
  local copies, waits for them, and re-layouts  3.18 us (3%)
    pallas_call x1, Pallas kernels, per_device(): pl.pallas_call(kernel, name='bond_apply', out_shape=(jax.ShapeDtypeStruct...  103 us

profile of v3, /device:TPU:1, one launch (start us, length us, event | category | flops | bytes accessed | tf_op | source)
XLA Modules:
  0.0 106.4 jit_solution(11580647001052927936)
XLA Ops:
  0.6 102.5 %bond_apply.1 = (bf16[64,32,128]{2,1,0:T(8,128)(2,1)}, f32[8,128]{1,0:T(8,128)}) custom-call(s32[96]{0:T(128)} %constant.2.clone.places, s32[64]{0:T(128)} %sector_left.1, s32[128]{0:T(128)} %left_sizes.1, s32[128]{0:T(128)} %right_sizes.1, s32[4096]{0:T(1024)} %my_right.1, s32[32,128]{1,0:T(8,128)} %bitcast.1, s32[4,64]{1,0:T(4,128)} %tmask.1, ...), custom_call_target="tpu_custom_call" | custom-call | tf_op jit(solution)/shard_map/bond_apply/pallas_call | solution.py:379
  103.2 1.3 %slice_reduce_fusion = f32[4]{0:T(128)} fusion(f32[8,128]{1,0:T(8,128)} %get-tuple-element.5), kind=kLoop, calls=%fused_computation | loop fusion | bytes 32 | tf_op jit(solution)/shard_map/slice | solution.py:434
  104.5 1.9 %copy.13 = bf16[64,32,128]{2,1,0:T(8,128)(2,1)} copy(bf16[64,32,128]{2,1,0:T(8,128)(2,1)} %get-tuple-element.8) | data formatting | bytes 1048576
